TPU v7x, 256 devices: a whole 4x4x8 slice. The times are simulated.
256 devices in a mesh: grp: 8 (over z_hi, core), blk: 32 (over x, y, z_lo).
Axes of the slice: x: 4, y: 4, z: 8 (z_hi: 4, z_lo: 2; z = z_hi * 2 + z_lo), core: 2. Of those that a mesh axis runs over, the one named last changes fastest.
Arguments:
- factors: bfloat16 [1024, 512, 512], P(('grp', 'blk')), may hold values from -6 to 6
- loadings: bfloat16 [512, 2048], replicated, may hold values from -0.25 to 0.25
- netload_map: bfloat16 [512, 200], replicated, may hold values from -0.25 to 0.25
- rule_weights: bfloat16 [32, 2048, 200], P('blk'), may hold values from -0.125 to 0.125
- rule_bias: float32 [32, 200], P('blk'), may hold values from -3 to 3
Outputs:
- decisions: bfloat16 [512, 1024, 200], P('blk', 'grp')
- rule_grad: float32 [32, 2048, 200], P('blk', 'grp')
All inputs are finite; a program needn't handle non-finite values.
Results may differ from a plain program's by a relative error of at most 0.01.
Values may be sent and summed in bfloat16 or wider, within the bound.
A program may use at most 128 MiB of HBM per device.

v0:
```python
import math
import jax
import jax.numpy as jnp
from jax import lax
from jax.sharding import PartitionSpec as P


def body(factors, loadings, netload_map, rule_weights, rule_bias):
    blocks = lax.axis_size("blk")
    groups = lax.axis_size("grp")
    path_dev, hours, width_k = factors.shape
    hour_blk = hours // blocks
    row_scale = 1.0 / math.sqrt(groups * blocks * path_dev * hour_blk)
    weights = rule_weights[0]
    offsets = rule_bias[0]
    ordered = jnp.transpose(factors.reshape(path_dev, blocks, hour_blk, width_k), (1, 2, 0, 3))
    features = jnp.tanh(
        jnp.einsum("...c,cf->...f", ordered, loadings, preferred_element_type=jnp.float32)
    ).astype(jnp.bfloat16)
    net_load = jnp.einsum(
        "...c,cd->...d", ordered, netload_map, preferred_element_type=jnp.float32
    ).astype(jnp.bfloat16)
    features, net_load = (features, net_load)
    decide_features = lax.all_to_all(features, "blk", split_axis=0, concat_axis=2, tiled=True)[0]
    decide_net_load = lax.all_to_all(net_load, "blk", split_axis=0, concat_axis=2, tiled=True)[0]
    dispatch = (
        jnp.einsum("krf,fd->krd", decide_features, weights, preferred_element_type=jnp.float32)
        + offsets
    )
    shortfall = decide_net_load.astype(jnp.float32) - dispatch
    slopes = (
        -4.0 * jax.nn.sigmoid(shortfall) + jax.nn.sigmoid(-shortfall) + 0.25 * dispatch
    ).astype(jnp.bfloat16)
    decisions, slopes, received = (dispatch.astype(jnp.bfloat16), slopes, decide_features)
    partial_grad = (
        jnp.einsum("krf,krd->fd", received, slopes, preferred_element_type=jnp.float32) * row_scale
    )[None]
    summed = lax.psum(partial_grad.astype(jnp.bfloat16), "grp").astype(jnp.float32)
    owned = partial_grad.shape[1] // groups
    grad_share = lax.dynamic_slice_in_dim(summed, lax.axis_index("grp") * owned, owned, 1)
    return (decisions, grad_share)


def solution(mesh):
    return jax.shard_map(
        body,
        mesh=mesh,
        in_specs=(P(("grp", "blk"), None, None), P(), P(), P("blk", None, None), P("blk", None)),
        out_specs=(P("blk", "grp", None), P("blk", "grp", None)),
        check_vma=False,
    )
```

profile of v0, /device:TPU:1, one launch (start us, length us, event | category | flops | bytes accessed | tf_op | source)
XLA Modules:
  0.0 289.5 jit_solution(17951146941334778530)
XLA Ops:
  7.2 0.0 copy-start
  7.2 3.4 %fusion.9 = bf16[32,16,4,200]{3,1,2,0:T(8,128)(2,1)} fusion(bf16[4,32,16,512]{3,2,1,0:T(8,128)(2,1)} %bitcast.49, bf16[512,200]{0,1:T(8,128)(2,1)} %param.7), kind=kOutput, calls=%fused_computation.13 | convolution fusion | flops 419840000 | bytes 3121152 | tf_op jit(solution)/shard_map/...c,cd->...d/dot_general | solution.py:20
  10.6 9.2 %all-to-all-start.1 = ((bf16[32,16,4,200]{3,1,2,0:T(8,128)(2,1)}), bf16[32,16,4,200]{3,1,2,0:T(8,128)(2,1)S(1)}, u32[]{:S(2)}, u32[]{:S(2)}) async-start(bf16[32,16,4,200]{3,1,2,0:T(8,128)(2,1)} %fusion.9), calls=%async_computation.1 | async-start | bytes 2097152 | tf_op jit(solution)/shard_map/all_to_all | solution.py:25
  19.8 0.0 copy-done
  19.8 8.3 %tanh_convert_fusion = bf16[32,16,4,2048]{3,1,2,0:T(8,128)(2,1)} fusion(bf16[512,2048]{1,0:T(8,128)(2,1)S(1)} %copy-done, bf16[4,32,16,512]{3,2,1,0:T(8,128)(2,1)} %bitcast.50), kind=kOutput, calls=%fused_computation | convolution fusion | flops 4299161600 | bytes 12582912 | tf_op jit(solution)/shard_map/...c,cf->...f/dot_general | solution.py:18
  28.2 8.4 %all-to-all-done.1 = bf16[32,16,4,200]{3,1,2,0:T(8,128)(2,1)S(1)} async-done(((bf16[32,16,4,200]{3,1,2,0:T(8,128)(2,1)}), bf16[32,16,4,200]{3,1,2,0:T(8,128)(2,1)S(1)}, u32[]{:S(2)}, u32[]{:S(2)}) %all-to-all-start.1) | async-done | bytes 819232 | tf_op jit(solution)/shard_map/all_to_all | solution.py:25
  36.6 5.0 %all-to-all-start = ((bf16[32,16,4,2048]{3,1,2,0:T(8,128)(2,1)}), bf16[32,16,4,2048]{3,1,2,0:T(8,128)(2,1)}, u32[]{:S(2)}, u32[]{:S(2)}) async-start(bf16[32,16,4,2048]{3,1,2,0:T(8,128)(2,1)} %tanh_convert_fusion), calls=%async_computation | async-start | bytes 16777216 | tf_op jit(solution)/shard_map/all_to_all | solution.py:24
  41.5 0.0 all-reduce.2.cloned.1.call-start
  41.6 1.6 bitcast_convert_fusion
  43.2 0.0 copy-start.2
  43.2 2.9 %copy.13 = f32[16,128,200]{1,2,0:T(8,128)} copy(f32[16,128,200]{2,0,1:T(8,128)} %bitcast.47) | data formatting | bytes 3276800 | tf_op jit(solution)/shard_map/convert_element_type | solution.py:30
  46.2 129.4 %all-to-all-done = bf16[32,16,4,2048]{3,1,2,0:T(8,128)(2,1)} async-done(((bf16[32,16,4,2048]{3,1,2,0:T(8,128)(2,1)}), bf16[32,16,4,2048]{3,1,2,0:T(8,128)(2,1)}, u32[]{:S(2)}, u32[]{:S(2)}) %all-to-all-start) | async-done | bytes 8388640 | tf_op jit(solution)/shard_map/all_to_all | solution.py:24
  175.6 0.0 copy-done.2
  175.6 7.1 %fusion.12 = f32[16,128,200]{2,0,1:T(8,128)} fusion(bf16[16,128,2048]{2,0,1:T(8,128)(2,1)} %bitcast.6, bf16[1,2048,200]{1,2,0:T(8,128)(2,1)S(1)} %copy-done.2), kind=kOutput, calls=%fused_computation.15 | convolution fusion | flops 1677721600 | bytes 10846208 | tf_op jit(solution)/shard_map/krf,fd->krd/dot_general | solution.py:27
  182.7 0.0 copy-start.1
  182.7 2.9 copy.17
  185.6 0.0 copy-done.1
  185.6 3.7 %add_convert_fusion = (bf16[16,128,200]{1,2,0:T(8,128)(2,1)S(1)}, bf16[16,128,200]{1,2,0:T(8,128)(2,1)}) fusion(f32[16,128,200]{1,2,0:T(8,128)} %copy.13, f32[16,128,200]{1,2,0:T(8,128)} %copy.17, f32[200]{0:T(256)S(1)} %bitcast.48), kind=kLoop, calls=%fused_computation.11 | loop fusion | flops 5324800 | bytes 4916000 | tf_op jit(solution)/shard_map/convert_element_type | solution.py:33
  189.3 1.7 copy.20
  191.0 6.4 %fusion.2 = bf16[1,2048,200]{1,2,0:T(8,128)(2,1)} fusion(bf16[16,128,2048]{2,0,1:T(8,128)(2,1)} %bitcast.6, bf16[16,128,200]{2,0,1:T(8,128)(2,1)} %copy.20), kind=kOutput, calls=%fused_computation.4 | convolution fusion | flops 1678540800 | bytes 10027008 | tf_op jit(solution)/shard_map/krf,krd->fd/dot_general | solution.py:36
  197.4 0.0 all-reduce.2.cloned.1.call-update
  197.4 83.7 %all-reduce.2.cloned.1.call-done = bf16[1,2048,200]{1,2,0:T(8,128)(2,1)} async-done(((bf16[1,2048,200]{1,2,0:T(8,128)(2,1)}), bf16[1,2048,200]{1,2,0:T(8,128)(2,1)}) %all-reduce.2.cloned.1.call-update) | async-done | bytes 819216 | tf_op jit(solution)/shard_map/psum | solution.py:38
  281.1 1.6 dynamic-slice_convert_fusion
Async XLA Ops:
  7.2 12.7 %copy-start = (bf16[512,2048]{1,0:T(8,128)(2,1)S(1)}, bf16[512,2048]{1,0:T(8,128)(2,1)}, u32[]{:S(2)}) copy-start(bf16[512,2048]{1,0:T(8,128)(2,1)} %param.6) | copy-start | bytes 6291460
  10.6 25.9 %all-to-all-start.1 = ((bf16[32,16,4,200]{3,1,2,0:T(8,128)(2,1)}), bf16[32,16,4,200]{3,1,2,0:T(8,128)(2,1)S(1)}, u32[]{:S(2)}, u32[]{:S(2)}) async-start(bf16[32,16,4,200]{3,1,2,0:T(8,128)(2,1)} %fusion.9), calls=%async_computation.1 | async-start | bytes 2097152 | tf_op jit(solution)/shard_map/all_to_all | solution.py:25
  36.6 139.0 %all-to-all-start = ((bf16[32,16,4,2048]{3,1,2,0:T(8,128)(2,1)}), bf16[32,16,4,2048]{3,1,2,0:T(8,128)(2,1)}, u32[]{:S(2)}, u32[]{:S(2)}) async-start(bf16[32,16,4,2048]{3,1,2,0:T(8,128)(2,1)} %tanh_convert_fusion), calls=%async_computation | async-start | bytes 16777216 | tf_op jit(solution)/shard_map/all_to_all | solution.py:24
  41.5 239.6 %all-reduce.2.cloned.1.call-start = ((), (), s32[]{:S(2)}) async-start(), calls=%async_computation.2 | async-start | bytes 1638400 | tf_op jit(solution)/shard_map/psum | solution.py:38
  43.2 132.4 %copy-start.2 = (bf16[1,2048,200]{1,2,0:T(8,128)(2,1)S(1)}, bf16[1,2048,200]{1,2,0:T(8,128)(2,1)}, u32[]{:S(2)}) copy-start(bf16[1,2048,200]{1,2,0:T(8,128)(2,1)} %param.8) | copy-start | bytes 2457604
  182.7 2.9 copy-start.1
Sparse Core Ops, SparseCore 0:
  197.5 83.5 all-reduce.1
where the time goes:
time: 290 us
  waiting for transfers between devices  222 us (77%)
  matrix products  25.3 us (9%)
  starting transfers between devices  14.2 us (5%)
  between operations  14.1 us (5%)
  local copies, waits for them, and re-layouts  7.5 us (3%)
  other arithmetic  6.93 us (2%)
    all_to_all x1, waiting for transfers between devices, body(): lax.all_to_all(features, 'blk', split_axis=0, concat_axis=2, tiled=True)[0]  129 us
    psum x1, waiting for transfers between devices, body(): lax.psum(partial_grad.astype(jnp.bfloat16), 'grp').astype(jnp.float32)  83.7 us
    all_to_all x1, starting transfers between devices, body(): lax.all_to_all(net_load, 'blk', split_axis=0, concat_axis=2, tiled=True)[0]  9.21 us
    all_to_all x1, waiting for transfers between devices, body(): lax.all_to_all(net_load, 'blk', split_axis=0, concat_axis=2, tiled=True)[0]  8.41 us
    dot_general x1, matrix products, body(): jnp.einsum('...c,cf->...f', ordered, loadings, preferred_element_type=jnp...  8.32 us
    dot_general x1, matrix products, body(): jnp.einsum('krf,fd->krd', decide_features, weights, preferred_element_typ...  7.12 us
    dot_general x1, matrix products, body(): jnp.einsum('krf,krd->fd', received, slopes, preferred_element_type=jnp.fl...  6.41 us
  transfers between devices with their start and end apart: 3, of which 3 were waited for; matrix products, arithmetic and copies ran while one was open for 4% of the time, Pallas kernels for 0%

commit v1 on v0

--- a/solution.py
+++ b/solution.py
@@ -35,7 +35,9 @@
     partial_grad = (
         jnp.einsum("krf,krd->fd", received, slopes, preferred_element_type=jnp.float32) * row_scale
     )[None]
-    summed = lax.psum(partial_grad.astype(jnp.bfloat16), "grp").astype(jnp.float32)
+    summed = jnp.sum(lax.all_gather(partial_grad.astype(jnp.bfloat16), axis_name="grp"), 0).astype(
+        jnp.float32
+    )
     owned = partial_grad.shape[1] // groups
     grad_share = lax.dynamic_slice_in_dim(summed, lax.axis_index("grp") * owned, owned, 1)
     return (decisions, grad_share)

time: 290 us -> 300 us (1.034)
  local copies, waits for them, and re-layouts: 7.5 us -> 14.9 us
  other arithmetic: 6.93 us -> 11.8 us
  waiting for transfers between devices: 222 us -> 219 us
    psum x1 -> x0, waiting for transfers between devices: 83.7 us -> none  [body(): lax.psum(partial_grad.astype(jnp.bfloat16), 'grp').astype(jnp.float32)]
    all_gather x0 -> x1, waiting for transfers between devices: none -> 81.2 us  [body(): lax.all_gather(partial_grad.astype(jnp.bfloat16), axis_name='grp')]
    unnamed x6 -> x7, local copies, waits for them, and re-layouts: 0.02 us -> 7.39 us
    reduce_sum x0 -> x1, other arithmetic: none -> 5.73 us  [body(): jnp.sum(lax.all_gather(partial_grad.astype(jnp.bfloat16), axis_name='grp'...]
where the time goes in v1:
time: 300 us; the launch traced here: 299 us
  waiting for transfers between devices  219 us (73%)
  matrix products  25.3 us (8%)
  local copies, waits for them, and re-layouts  14.9 us (5%)
  starting transfers between devices  14.2 us (5%)
  between operations  14.1 us (5%)
  other arithmetic  11.8 us (4%)
    all_to_all x1, waiting for transfers between devices, body(): lax.all_to_all(features, 'blk', split_axis=0, concat_axis=2, tiled=True)[0]  129 us
    all_gather x1, waiting for transfers between devices, body(): lax.all_gather(partial_grad.astype(jnp.bfloat16), axis_name='grp')  81.2 us
    all_to_all x1, starting transfers between devices, body(): lax.all_to_all(net_load, 'blk', split_axis=0, concat_axis=2, tiled=True)[0]  9.21 us
    all_to_all x1, waiting for transfers between devices, body(): lax.all_to_all(net_load, 'blk', split_axis=0, concat_axis=2, tiled=True)[0]  8.4 us
    dot_general x1, matrix products, body(): jnp.einsum('...c,cf->...f', ordered, loadings, preferred_element_type=jnp...  8.31 us
    unnamed x7, local copies, waits for them, and re-layouts  7.39 us
    dot_general x1, matrix products, body(): jnp.einsum('krf,fd->krd', decide_features, weights, preferred_element_typ...  7.12 us
    dot_general x1, matrix products, body(): jnp.einsum('krf,krd->fd', received, slopes, preferred_element_type=jnp.fl...  6.42 us
  transfers between devices with their start and end apart: 3, of which 3 were waited for; matrix products, arithmetic and copies ran while one was open for 4% of the time, Pallas kernels for 0%

profile of v1, /device:TPU:1, one launch (start us, length us, event | category | flops | bytes accessed | tf_op | source)
XLA Modules:
  0.0 299.2 jit_solution(1903493360762272389)
XLA Ops:
  7.2 0.0 copy-start
  7.2 3.4 %fusion.8 = bf16[32,16,4,200]{3,1,2,0:T(8,128)(2,1)} fusion(bf16[4,32,16,512]{3,2,1,0:T(8,128)(2,1)} %bitcast.53, bf16[512,200]{0,1:T(8,128)(2,1)} %param.7), kind=kOutput, calls=%fused_computation.13 | convolution fusion | flops 419840000 | bytes 3121152 | tf_op jit(solution)/shard_map/...c,cd->...d/dot_general | solution.py:20
  10.6 9.2 %all-to-all-start.1 = ((bf16[32,16,4,200]{3,1,2,0:T(8,128)(2,1)}), bf16[32,16,4,200]{3,1,2,0:T(8,128)(2,1)S(1)}, u32[]{:S(2)}, u32[]{:S(2)}) async-start(bf16[32,16,4,200]{3,1,2,0:T(8,128)(2,1)} %fusion.8), calls=%async_computation.1 | async-start | bytes 2097152 | tf_op jit(solution)/shard_map/all_to_all | solution.py:25
  19.8 0.0 copy-done
  19.8 8.3 %tanh_convert_fusion = bf16[32,16,4,2048]{3,1,2,0:T(8,128)(2,1)} fusion(bf16[512,2048]{1,0:T(8,128)(2,1)S(1)} %copy-done, bf16[4,32,16,512]{3,2,1,0:T(8,128)(2,1)} %bitcast.54), kind=kOutput, calls=%fused_computation | convolution fusion | flops 4299161600 | bytes 12582912 | tf_op jit(solution)/shard_map/...c,cf->...f/dot_general | solution.py:18
  28.2 8.4 %all-to-all-done.1 = bf16[32,16,4,200]{3,1,2,0:T(8,128)(2,1)S(1)} async-done(((bf16[32,16,4,200]{3,1,2,0:T(8,128)(2,1)}), bf16[32,16,4,200]{3,1,2,0:T(8,128)(2,1)S(1)}, u32[]{:S(2)}, u32[]{:S(2)}) %all-to-all-start.1) | async-done | bytes 819232 | tf_op jit(solution)/shard_map/all_to_all | solution.py:25
  36.6 5.0 %all-to-all-start = ((bf16[32,16,4,2048]{3,1,2,0:T(8,128)(2,1)}), bf16[32,16,4,2048]{3,1,2,0:T(8,128)(2,1)}, u32[]{:S(2)}, u32[]{:S(2)}) async-start(bf16[32,16,4,2048]{3,1,2,0:T(8,128)(2,1)} %tanh_convert_fusion), calls=%async_computation | async-start | bytes 16777216 | tf_op jit(solution)/shard_map/all_to_all | solution.py:24
  41.5 0.0 all-gather.3.cloned.1.call-start
  41.6 1.6 bitcast_convert_fusion
  43.2 0.0 copy-start.2
  43.2 2.9 copy.13
  46.2 129.3 %all-to-all-done = bf16[32,16,4,2048]{3,1,2,0:T(8,128)(2,1)} async-done(((bf16[32,16,4,2048]{3,1,2,0:T(8,128)(2,1)}), bf16[32,16,4,2048]{3,1,2,0:T(8,128)(2,1)}, u32[]{:S(2)}, u32[]{:S(2)}) %all-to-all-start) | async-done | bytes 8388640 | tf_op jit(solution)/shard_map/all_to_all | solution.py:24
  175.5 0.0 copy-done.2
  175.5 7.1 %fusion.11 = f32[16,128,200]{2,0,1:T(8,128)} fusion(bf16[16,128,2048]{2,0,1:T(8,128)(2,1)} %bitcast.6, bf16[1,2048,200]{1,2,0:T(8,128)(2,1)S(1)} %copy-done.2), kind=kOutput, calls=%fused_computation.15 | convolution fusion | flops 1677721600 | bytes 10846208 | tf_op jit(solution)/shard_map/krf,fd->krd/dot_general | solution.py:27
  182.6 0.0 copy-start.1
  182.6 2.9 copy.17
  185.5 0.0 copy-done.1
  185.5 3.7 %add_convert_fusion = (bf16[16,128,200]{1,2,0:T(8,128)(2,1)S(1)}, bf16[16,128,200]{1,2,0:T(8,128)(2,1)}) fusion(f32[16,128,200]{1,2,0:T(8,128)} %copy.13, f32[16,128,200]{1,2,0:T(8,128)} %copy.17, f32[200]{0:T(256)S(1)} %bitcast.52), kind=kLoop, calls=%fused_computation.11 | loop fusion | flops 5324800 | bytes 4916000 | tf_op jit(solution)/shard_map/convert_element_type | solution.py:33
  189.2 1.7 copy.20
  190.9 6.4 %fusion.1 = bf16[2048,200]{0,1:T(8,128)(2,1)} fusion(bf16[16,128,2048]{2,0,1:T(8,128)(2,1)} %bitcast.6, bf16[16,128,200]{2,0,1:T(8,128)(2,1)} %copy.20), kind=kOutput, calls=%fused_computation.4 | convolution fusion | flops 1678540800 | bytes 10027008 | tf_op jit(solution)/shard_map/krf,krd->fd/dot_general | solution.py:36
  197.3 0.0 all-gather.3.cloned.1.call-update
  197.3 81.2 %all-gather.3.cloned.1.call-done = bf16[16384,200]{0,1:T(8,128)(2,1)} async-done(((bf16[2048,200]{0,1:T(8,128)(2,1)}), bf16[16384,200]{0,1:T(8,128)(2,1)}) %all-gather.3.cloned.1.call-update) | async-done | bytes 6553616 | tf_op jit(solution)/shard_map/all_gather | solution.py:38
  278.5 7.4 %copy.21 = bf16[25,8,8,2048]{3,2,1,0:T(8,128)(2,1)S(1)} copy(bf16[25,8,8,2048]{3,1,2,0:T(8,128)(2,1)} %bitcast.51) | data formatting | bytes 13107200
  285.9 5.7 %bitcast_reduce_fusion = bf16[2048,200]{0,1:T(8,128)(2,1)S(1)} fusion(bf16[25,8,8,2048]{3,2,1,0:T(8,128)(2,1)S(1)} %copy.21), kind=kLoop, calls=%fused_computation.1 | loop fusion | flops 2867200 | bytes 7372800 | tf_op jit(solution)/shard_map/reduce_sum | solution.py:38
  291.6 0.7 convert_bitcast_fusion
Async XLA Ops:
  7.2 12.7 %copy-start = (bf16[512,2048]{1,0:T(8,128)(2,1)S(1)}, bf16[512,2048]{1,0:T(8,128)(2,1)}, u32[]{:S(2)}) copy-start(bf16[512,2048]{1,0:T(8,128)(2,1)} %param.6) | copy-start | bytes 6291460
  10.6 25.9 %all-to-all-start.1 = ((bf16[32,16,4,200]{3,1,2,0:T(8,128)(2,1)}), bf16[32,16,4,200]{3,1,2,0:T(8,128)(2,1)S(1)}, u32[]{:S(2)}, u32[]{:S(2)}) async-start(bf16[32,16,4,200]{3,1,2,0:T(8,128)(2,1)} %fusion.8), calls=%async_computation.1 | async-start | bytes 2097152 | tf_op jit(solution)/shard_map/all_to_all | solution.py:25
  36.6 138.9 %all-to-all-start = ((bf16[32,16,4,2048]{3,1,2,0:T(8,128)(2,1)}), bf16[32,16,4,2048]{3,1,2,0:T(8,128)(2,1)}, u32[]{:S(2)}, u32[]{:S(2)}) async-start(bf16[32,16,4,2048]{3,1,2,0:T(8,128)(2,1)} %tanh_convert_fusion), calls=%async_computation | async-start | bytes 16777216 | tf_op jit(solution)/shard_map/all_to_all | solution.py:24
  41.5 237.0 %all-gather.3.cloned.1.call-start = ((), (), s32[]{:S(2)}) async-start(), calls=%async_computation.2 | async-start | bytes 7372800 | tf_op jit(solution)/shard_map/all_gather | solution.py:38
  43.2 132.3 %copy-start.2 = (bf16[1,2048,200]{1,2,0:T(8,128)(2,1)S(1)}, bf16[1,2048,200]{1,2,0:T(8,128)(2,1)}, u32[]{:S(2)}) copy-start(bf16[1,2048,200]{1,2,0:T(8,128)(2,1)} %param.8) | copy-start | bytes 2457604
  182.6 2.9 copy-start.1
Sparse Core Ops, SparseCore 0:
  197.4 81.0 all-gather.2
